TPU v7x, 32 devices: a whole 2x2x4 slice. The times are simulated.
32 devices in a mesh: leaf: 16 (over z, y, x), panel: 2 (over core).
Axes of the slice: x: 2, y: 2, z: 4, core: 2. Of those that a mesh axis runs over, the one named last changes fastest.
Arguments:
- child_front: bfloat16 [4096, 16384], P('leaf', 'panel'), may hold values from -6 to 6
- own_map: int32 [3, 16, 2], P(None, 'leaf'), may hold values from 0 to 1, each once within a row
- cross_map: int32 [3, 16, 2], P(None, 'leaf'), may hold values from 0 to 1, each once within a row
- pivot_inverse: bfloat16 [7, 512, 512], replicated, may hold values from -0.0029296875 to 0.0029296875
Outputs:
- schur: bfloat16 [4096, 16384], P('leaf', 'panel')
Inputs may be any that keep to these rules, and one draw needn't show every extreme that they name: Each own_map[k, d, :] is a permutation of the 2 blocks. Each cross_map[k, d, :] is a permutation of the 2 blocks.
All inputs are finite; a program needn't handle non-finite values.
Results may differ from a plain program's by a relative error of at most 0.0088.
Values may be sent and summed in bfloat16 or wider, within the bound.
No kernel may reach another device: no remote copies, remote signals or barrier semaphores. Data moves between devices by JAX's collectives and lax.ppermute only.
A program may use at most 64 MiB of HBM per device.

v0:
```python
import jax
import jax.numpy as jnp
from jax import lax
from jax.sharding import PartitionSpec as P

PANEL = 512
BLOCK = 128


def swapped(block, axis, stride):
    count = lax.axis_size(axis)
    route = []
    for low in range(count):
        high = low | 1 << stride
        if high != low and high < count:
            route += [(low, high), (high, low)]
    return lax.ppermute(block, axis, route)


def spread(block, axis, owner):
    block = jnp.where(lax.axis_index(axis) == owner, block, jnp.zeros_like(block))
    return lax.psum(block, axis)


def extend_add(front_slab, partner, own_index, cross_index, block_count):
    slab_cols = front_slab.shape[1]
    slots = jnp.arange(block_count, dtype=jnp.int32)[None, :]
    own_table = (own_index[:, None] == slots).astype(jnp.bfloat16)
    cross_table = (cross_index[:, None] == slots).astype(jnp.bfloat16)
    own_blocks = front_slab.reshape(block_count, BLOCK, slab_cols)
    cross_blocks = partner.reshape(block_count, BLOCK, slab_cols)
    summed = jnp.einsum("sb,brc->src", own_table, own_blocks, preferred_element_type=jnp.float32)
    summed = summed + jnp.einsum(
        "sb,brc->src", cross_table, cross_blocks, preferred_element_type=jnp.float32
    )
    return summed.reshape(block_count * BLOCK, slab_cols).astype(jnp.bfloat16)


def collect_pivots(own_rows, leaf_index, group_bits):
    buffer = own_rows
    for step_bit in range(group_bits):
        received = swapped(buffer, "leaf", step_bit)
        upper_half = leaf_index >> step_bit & 1 == 1
        buffer = jnp.where(
            upper_half,
            jnp.concatenate([received, buffer], axis=0),
            jnp.concatenate([buffer, received], axis=0),
        )
    return buffer


def top_upper(own_rows, inverse):
    product = jnp.dot(
        inverse,
        lax.all_gather(own_rows, "leaf", axis=0, tiled=True),
        preferred_element_type=jnp.float32,
    )
    return product.astype(jnp.bfloat16)


def on_device(child_front, own_map, cross_map, pivot_inverse):
    leaf_count = lax.axis_size("leaf")
    leaf_bits = leaf_count.bit_length() - 1
    leaf_index = lax.axis_index("leaf")
    slab_rows = child_front.shape[0]
    block_count = slab_rows // BLOCK
    front_slab = child_front
    offsets = (0, 4, 6)
    for level_index in range(3):
        group_size = leaf_count // 2 ** (2 - level_index)
        group_bits = leaf_bits - 2 + level_index
        share_rows = PANEL // group_size
        partner = swapped(front_slab, "leaf", group_bits - 1)
        parent = extend_add(
            front_slab, partner, own_map[level_index, 0], cross_map[level_index, 0], block_count
        )
        front_number = offsets[level_index] + leaf_index // group_size
        inverse = lax.dynamic_index_in_dim(pivot_inverse, front_number, 0, keepdims=False)
        own_rows = parent[:share_rows]
        if level_index < 2:
            pivots = collect_pivots(own_rows, leaf_index, group_bits)
            upper_rows = jnp.dot(inverse, pivots, preferred_element_type=jnp.float32).astype(
                jnp.bfloat16
            )
        else:
            upper_rows = top_upper(own_rows, inverse)
        columns = spread(parent[:, :PANEL], "panel", 0)
        reduced = parent.astype(jnp.float32) - jnp.dot(
            columns, upper_rows, preferred_element_type=jnp.float32
        )
        keep_mask = jnp.arange(slab_rows, dtype=jnp.int32)[:, None] >= share_rows
        front_slab = jnp.where(keep_mask, reduced, jnp.zeros_like(reduced)).astype(jnp.bfloat16)
    return front_slab


def solution(mesh):
    placed = (P("leaf", "panel"), P(None, "leaf", None), P(None, "leaf", None), P())
    return jax.shard_map(
        on_device, mesh=mesh, in_specs=placed, out_specs=P("leaf", "panel"), check_vma=False
    )
```

profile of v0, /device:TPU:0, one launch (start us, length us, event | category | flops | bytes accessed | tf_op | source)
XLA Modules:
  0.0 882.2 jit_solution(7611758241214529252)
XLA Ops:
  6.5 3.0 collective-permute-start
  9.5 1.0 slice_reduce_fusion.5
  10.5 1.0 slice_reduce_fusion
  11.5 10.0 %fusion.28 = f32[2,128,8192]{2,0,1:T(2,128)S(1)} fusion(bf16[2,128,8192]{2,1,0:T(8,128)(2,1)} %bitcast.58, s32[2]{0:T(128)S(1)} %get-tuple-element.9), kind=kOutput, calls=%fused_computation.41 | convolution fusion | flops 8388612 | bytes 12582920 | tf_op jit(solution)/shard_map/sb,brc->src/dot_general | solution.py:32
  21.6 78.7 %collective-permute-done = bf16[256,8192]{1,0:T(8,128)(2,1)S(1)} collective-permute-done((bf16[256,8192]{1,0:T(8,128)(2,1)}, bf16[256,8192]{1,0:T(8,128)(2,1)S(1)}, u32[]{:S(2)}, u32[]{:S(2)}) %collective-permute-start) | collective-permute-done | bytes 4194336 | tf_op jit(solution)/shard_map/ppermute | solution.py:17
  100.3 8.1 fusion.3
  108.4 2.0 copy-done
  110.4 2.3 copy.35
  112.7 1.8 collective-permute-start.1
  114.5 45.2 %collective-permute-done.1 = bf16[128,8192]{1,0:T(8,128)(2,1)} collective-permute-done((bf16[128,8192]{1,0:T(8,128)(2,1)S(1)}, bf16[128,8192]{1,0:T(8,128)(2,1)}, u32[]{:S(2)}, u32[]{:S(2)}) %collective-permute-start.1) | collective-permute-done | bytes 2097184 | tf_op jit(solution)/shard_map/ppermute | solution.py:17
  159.7 4.5 maximum_select_fusion.8
  164.2 1.5 collective-permute-start.2
  165.7 4.9 copy.14
  170.6 2.0 copy-done.3
  172.6 0.7 slice_select_fusion.2
  173.3 0.0 all-reduce.6.cloned.1.call-start
  173.4 18.6 %all-reduce.4.cloned.1.call-done = bf16[256,512]{1,0:T(8,128)(2,1)} async-done(((bf16[256,512]{1,0:T(8,128)(2,1)}), bf16[256,512]{1,0:T(8,128)(2,1)}) %all-reduce.4.cloned.1.call-update) | async-done | bytes 262160 | tf_op jit(solution)/shard_map/psum | solution.py:22
  192.0 63.4 %collective-permute-done.2 = bf16[256,8192]{1,0:T(8,128)(2,1)} collective-permute-done((bf16[256,8192]{1,0:T(8,128)(2,1)}, bf16[256,8192]{1,0:T(8,128)(2,1)}, u32[]{:S(2)}, u32[]{:S(2)}) %collective-permute-start.2) | collective-permute-done | bytes 4194336 | tf_op jit(solution)/shard_map/ppermute | solution.py:17
  255.4 12.8 %fusion.8 = bf16[256,8192]{1,0:T(8,128)(2,1)} fusion(bf16[256,512]{1,0:T(8,128)(2,1)} %all-reduce.4.cloned.1.call-done, bf16[256,8192]{1,0:T(8,128)(2,1)} %bitcast.57, bf16[256,8192]{1,0:T(8,128)(2,1)} %maximum_select_fusion.8, bf16[256,8192]{1,0:T(8,128)(2,1)} %collective-permute-done.2, pred[]{:T(512)S(6)} %eq.123, ...), kind=kOutput, calls=%fused_computation.17 | convolution fusion | flops 6492782592 | bytes 17563908 | tf_op jit(solution)/shard_map/dot_general | solution.py:88
  268.2 1.2 collective-permute-start.3
  269.4 10.0 %fusion.25 = f32[2,128,8192]{2,0,1:T(2,128)S(1)} fusion(bf16[2,128,8192]{2,1,0:T(8,128)(2,1)} %bitcast.61, s32[2]{0:T(128)S(1)} %get-tuple-element.10), kind=kOutput, calls=%fused_computation.38 | convolution fusion | flops 8388612 | bytes 12582920 | tf_op jit(solution)/shard_map/sb,brc->src/dot_general | solution.py:32
  279.5 78.9 %collective-permute-done.3 = bf16[256,8192]{1,0:T(8,128)(2,1)S(1)} collective-permute-done((bf16[256,8192]{1,0:T(8,128)(2,1)}, bf16[256,8192]{1,0:T(8,128)(2,1)S(1)}, u32[]{:S(2)}, u32[]{:S(2)}) %collective-permute-start.3) | collective-permute-done | bytes 4194336 | tf_op jit(solution)/shard_map/ppermute | solution.py:17
  358.4 8.1 fusion.4
  366.5 2.7 copy.17
  369.2 0.1 slice.55
  369.3 0.9 collective-permute-start.4
  370.3 20.9 %collective-permute-done.4 = bf16[64,8192]{1,0:T(8,128)(2,1)S(1)} collective-permute-done((bf16[64,8192]{1,0:T(8,128)(2,1)S(1)}, bf16[64,8192]{1,0:T(8,128)(2,1)S(1)}, u32[]{:S(2)}, u32[]{:S(2)}) %collective-permute-start.4) | collective-permute-done | bytes 1048608 | tf_op jit(solution)/shard_map/ppermute | solution.py:17
  391.1 0.4 maximum_select_fusion.10
  391.6 0.7 collective-permute-start.5
  392.3 42.7 %collective-permute-done.5 = bf16[128,8192]{1,0:T(8,128)(2,1)S(1)} collective-permute-done((bf16[128,8192]{1,0:T(8,128)(2,1)S(1)}, bf16[128,8192]{1,0:T(8,128)(2,1)S(1)}, u32[]{:S(2)}, u32[]{:S(2)}) %collective-permute-start.5) | collective-permute-done | bytes 2097184 | tf_op jit(solution)/shard_map/ppermute | solution.py:17
  435.0 3.2 maximum_select_fusion.9
  438.2 0.4 collective-permute-start.6
  438.6 0.7 slice_select_fusion.1
  439.3 0.0 all-reduce.8.cloned.1.call-start
  439.4 18.5 %all-reduce.6.cloned.1.call-done = bf16[256,512]{1,0:T(8,128)(2,1)} async-done(((bf16[256,512]{1,0:T(8,128)(2,1)}), bf16[256,512]{1,0:T(8,128)(2,1)}) %all-reduce.6.cloned.1.call-update) | async-done | bytes 262160 | tf_op jit(solution)/shard_map/psum | solution.py:22
  458.0 68.0 %collective-permute-done.6 = bf16[256,8192]{1,0:T(8,128)(2,1)} collective-permute-done((bf16[256,8192]{1,0:T(8,128)(2,1)}, bf16[256,8192]{1,0:T(8,128)(2,1)}, u32[]{:S(2)}, u32[]{:S(2)}) %collective-permute-start.6) | collective-permute-done | bytes 4194336 | tf_op jit(solution)/shard_map/ppermute | solution.py:17
  526.0 12.6 %fusion.7 = bf16[256,8192]{1,0:T(8,128)(2,1)} fusion(bf16[256,512]{1,0:T(8,128)(2,1)} %all-reduce.6.cloned.1.call-done, bf16[256,8192]{1,0:T(8,128)(2,1)} %bitcast.52, bf16[256,8192]{1,0:T(8,128)(2,1)} %maximum_select_fusion.9, bf16[256,8192]{1,0:T(8,128)(2,1)} %collective-permute-done.6, pred[]{:T(512)S(6)} %eq.129, ...), kind=kOutput, calls=%fused_computation.16 | convolution fusion | flops 6492782592 | bytes 17563908 | tf_op jit(solution)/shard_map/dot_general | solution.py:88
  538.5 1.2 collective-permute-start.7
  539.7 10.0 %fusion.22 = f32[2,128,8192]{2,0,1:T(2,128)S(1)} fusion(bf16[2,128,8192]{2,1,0:T(8,128)(2,1)} %bitcast.60, s32[2]{0:T(128)S(1)} %get-tuple-element.8), kind=kOutput, calls=%fused_computation.35 | convolution fusion | flops 8388612 | bytes 12582920 | tf_op jit(solution)/shard_map/sb,brc->src/dot_general | solution.py:32
  549.7 166.0 %collective-permute-done.7 = bf16[256,8192]{1,0:T(8,128)(2,1)S(1)} collective-permute-done((bf16[256,8192]{1,0:T(8,128)(2,1)}, bf16[256,8192]{1,0:T(8,128)(2,1)S(1)}, u32[]{:S(2)}, u32[]{:S(2)}) %collective-permute-start.7) | collective-permute-done | bytes 4194336 | tf_op jit(solution)/shard_map/ppermute | solution.py:17
  715.7 8.1 fusion.5
  723.8 2.7 copy.20
  726.5 2.0 copy-done.2
  728.5 0.7 slice_select_fusion
  729.3 1.9 slice.57
  731.3 16.2 %all-reduce.8.cloned.1.call-done = bf16[256,512]{1,0:T(8,128)(2,1)} async-done(((bf16[256,512]{1,0:T(8,128)(2,1)}), bf16[256,512]{1,0:T(8,128)(2,1)}) %all-reduce.8.cloned.1.call-update) | async-done | bytes 262160 | tf_op jit(solution)/shard_map/psum | solution.py:22
  747.5 116.2 %all-gather.2.cloned.1.call-done = bf16[512,8192]{1,0:T(8,128)(2,1)} async-done(((bf16[32,8192]{1,0:T(8,128)(2,1)}), bf16[512,8192]{1,0:T(8,128)(2,1)}) %all-gather.2.cloned.1.call-update) | async-done | bytes 8388624 | tf_op jit(solution)/shard_map/all_gather | solution.py:55
  863.7 11.5 %fusion.6 = bf16[256,8192]{1,0:T(8,128)(2,1)} fusion(bf16[256,512]{1,0:T(8,128)(2,1)} %all-reduce.8.cloned.1.call-done, bf16[256,8192]{1,0:T(8,128)(2,1)} %bitcast.55, pred[256]{0:T(512)(128)(4,1)S(1)} %iota_compare_fusion.2, bf16[512,8192]{1,0:T(8,128)(2,1)} %all-gather.2.cloned.1.call-done, bf16[7,512,512]{2,1,0:T(8,128)(2,1)} %param.7, s32[]{:T(128)S(6)} %select_n.104), kind=kOutput, calls=%fused_computation.15 | convolution fusion | flops 6455033856 | bytes 17563908 | tf_op jit(solution)/shard_map/dot_general | solution.py:88
  (14 shorter events, 0.1 us)
Async XLA Ops:
  6.5 185.5 %all-reduce.4.cloned.1.call-start = ((), (), s32[]{:S(2)}) async-start(), calls=%async_computation | async-start | bytes 524288 | tf_op jit(solution)/shard_map/psum | solution.py:22
  6.5 93.8 %collective-permute-start = (bf16[256,8192]{1,0:T(8,128)(2,1)}, bf16[256,8192]{1,0:T(8,128)(2,1)S(1)}, u32[]{:S(2)}, u32[]{:S(2)}) collective-permute-start(bf16[256,8192]{1,0:T(8,128)(2,1)} %param.4), channel_id=1, source_target_pairs={{0,4},{4,0},{2,6},{6,2},{8,12},{12,8},{10,14},{14,10},{16,20},{20,... | collective-permute-start | bytes 12582920 | tf_op jit(solution)/shard_map/ppermute | solution.py:17
  108.4 2.0 copy-start
  112.7 47.0 %collective-permute-start.1 = (bf16[128,8192]{1,0:T(8,128)(2,1)S(1)}, bf16[128,8192]{1,0:T(8,128)(2,1)}, u32[]{:S(2)}, u32[]{:S(2)}) collective-permute-start(bf16[128,8192]{1,0:T(8,128)(2,1)S(1)} %bitcast.48), channel_id=1, source_target_pairs={{0,2},{2,0},{4,6},{6,4},{8,10},{10,8},{12,14},{14,12},{16,18},{18,... | collective-permute-start | bytes 6291464 | tf_op jit(solution)/shard_map/ppermute | solution.py:17
  164.2 91.2 %collective-permute-start.2 = (bf16[256,8192]{1,0:T(8,128)(2,1)}, bf16[256,8192]{1,0:T(8,128)(2,1)}, u32[]{:S(2)}, u32[]{:S(2)}) collective-permute-start(bf16[256,8192]{1,0:T(8,128)(2,1)} %maximum_select_fusion.8), channel_id=1, source_target_pairs={{0,4},{4,0},{2,6},{6,2},{8,12},{12,8},{10,14},{14,10},{16,20},{20,... | collective-permute-start | bytes 12582920 | tf_op jit(solution)/shard_map/ppermute | solution.py:17
  170.6 2.0 copy-start.3
  173.3 284.6 %all-reduce.6.cloned.1.call-start = ((), (), s32[]{:S(2)}) async-start(), calls=%async_computation.1 | async-start | bytes 524288 | tf_op jit(solution)/shard_map/psum | solution.py:22
  268.2 90.2 %collective-permute-start.3 = (bf16[256,8192]{1,0:T(8,128)(2,1)}, bf16[256,8192]{1,0:T(8,128)(2,1)S(1)}, u32[]{:S(2)}, u32[]{:S(2)}) collective-permute-start(bf16[256,8192]{1,0:T(8,128)(2,1)} %fusion.8), channel_id=1, source_target_pairs={{0,8},{8,0},{2,10},{10,2},{4,12},{12,4},{6,14},{14,6},{16,24},{24,... | collective-permute-start | bytes 12582920 | tf_op jit(solution)/shard_map/ppermute | solution.py:17
  369.2 69.4 %copy-start.1 = (bf16[2,128,8192]{2,1,0:T(8,128)(2,1)}, bf16[2,128,8192]{2,1,0:T(8,128)(2,1)S(1)}, u32[]{:S(2)}) copy-start(bf16[2,128,8192]{2,1,0:T(8,128)(2,1)S(1)} %copy.17) | copy-start | bytes 12582916
  369.3 21.8 %collective-permute-start.4 = (bf16[64,8192]{1,0:T(8,128)(2,1)S(1)}, bf16[64,8192]{1,0:T(8,128)(2,1)S(1)}, u32[]{:S(2)}, u32[]{:S(2)}) collective-permute-start(bf16[64,8192]{1,0:T(8,128)(2,1)S(1)} %slice.55), channel_id=1, source_target_pairs={{0,2},{2,0},{4,6},{6,4},{8,10},{10,8},{12,14},{14,12},{16,18},{18,... | collective-permute-start | bytes 3145736 | tf_op jit(solution)/shard_map/ppermute | solution.py:17
  391.6 43.4 %collective-permute-start.5 = (bf16[128,8192]{1,0:T(8,128)(2,1)S(1)}, bf16[128,8192]{1,0:T(8,128)(2,1)S(1)}, u32[]{:S(2)}, u32[]{:S(2)}) collective-permute-start(bf16[128,8192]{1,0:T(8,128)(2,1)S(1)} %maximum_select_fusion.10), channel_id=1, source_target_pairs={{0,4},{4,0},{2,6},{6,2},{8,12},{12,8},{10,14},{14,10},{16,20},{20,... | collective-permute-start | bytes 6291464 | tf_op jit(solution)/shard_map/ppermute | solution.py:17
  438.2 87.8 %collective-permute-start.6 = (bf16[256,8192]{1,0:T(8,128)(2,1)}, bf16[256,8192]{1,0:T(8,128)(2,1)}, u32[]{:S(2)}, u32[]{:S(2)}) collective-permute-start(bf16[256,8192]{1,0:T(8,128)(2,1)} %maximum_select_fusion.9), channel_id=1, source_target_pairs={{0,8},{8,0},{2,10},{10,2},{4,12},{12,4},{6,14},{14,6},{16,24},{24,... | collective-permute-start | bytes 12582920 | tf_op jit(solution)/shard_map/ppermute | solution.py:17
  439.3 308.2 %all-reduce.8.cloned.1.call-start = ((), (), s32[]{:S(2)}) async-start(), calls=%async_computation.2 | async-start | bytes 524288 | tf_op jit(solution)/shard_map/psum | solution.py:22
  538.5 177.2 %collective-permute-start.7 = (bf16[256,8192]{1,0:T(8,128)(2,1)}, bf16[256,8192]{1,0:T(8,128)(2,1)S(1)}, u32[]{:S(2)}, u32[]{:S(2)}) collective-permute-start(bf16[256,8192]{1,0:T(8,128)(2,1)} %fusion.7), channel_id=1, source_target_pairs={{0,16},{16,0},{2,18},{18,2},{4,20},{20,4},{6,22},{22,6},{8,24},{24... | collective-permute-start | bytes 12582920 | tf_op jit(solution)/shard_map/ppermute | solution.py:17
  726.5 2.0 copy-start.2
  729.3 134.4 %all-gather.2.cloned.1.call-start = ((), (), s32[]{:S(2)}) async-start(), calls=%async_computation.3 | async-start | bytes 8912896 | tf_op jit(solution)/shard_map/all_gather | solution.py:55
Sparse Core Ops, SparseCore 0:
  173.4 18.5 all-reduce.3
  439.5 18.4 all-reduce.5
  729.4 18.0 all-reduce.7
  750.2 113.4 all-gather.1
where the time goes:
time: 891 us; the launch traced here: 882 us
  waiting for transfers between devices  733 us (82%)
  matrix products  91.3 us (10%)
  local copies, waits for them, and re-layouts  22.5 us (3%)
  between operations  13.8 us (2%)
  starting transfers between devices  10.8 us (1%)
  other arithmetic  10.4 us (1%)
    ppermute x8, waiting for transfers between devices, swapped(): return lax.ppermute(block, axis, route)  564 us
    all_gather x1, waiting for transfers between devices, top_upper(): lax.all_gather(own_rows, 'leaf', axis=0, tiled=True)  116 us
    psum x3, waiting for transfers between devices, spread(): return lax.psum(block, axis)  53.4 us
    dot_general x3, matrix products, on_device(): jnp.dot(columns, upper_rows, preferred_element_type=jnp.float32)  36.9 us
    dot_general x3, matrix products, extend_add(): jnp.einsum('sb,brc->src', own_table, own_blocks, preferred_element_type=j...  30.1 us
    dot_general x3, matrix products, extend_add(): jnp.einsum('sb,brc->src', cross_table, cross_blocks, preferred_element_ty...  24.3 us
  transfers between devices with their start and end apart: 12, of which 12 were waited for; matrix products, arithmetic and copies ran while one was open for 5% of the time, Pallas kernels for 0%

commit v1 on v0

--- a/solution.py
+++ b/solution.py
@@ -19,7 +19,7 @@
 
 def spread(block, axis, owner):
     block = jnp.where(lax.axis_index(axis) == owner, block, jnp.zeros_like(block))
-    return lax.psum(block, axis)
+    return jnp.sum(lax.all_gather(block, axis), axis=0)
 
 
 def extend_add(front_slab, partner, own_index, cross_index, block_count):

time: 891 us -> 869 us (0.975)
  waiting for transfers between devices: 733 us -> 706 us
    psum x3 -> x0, waiting for transfers between devices: 53.4 us -> none  [spread(): return lax.psum(block, axis)]
    ppermute x8, waiting for transfers between devices: 564 us -> 597 us  [swapped(): return lax.ppermute(block, axis, route)]
  transfers between devices with their start and end apart: 12 -> 9, of which waited for: 12 -> 9; matrix products, arithmetic and copies ran while one was open for 5% -> 5% of each run, Pallas kernels for 0% -> 0%
where the time goes in v1:
time: 869 us; the launch traced here: 860 us
  waiting for transfers between devices  706 us (81%)
  matrix products  90.9 us (10%)
  local copies, waits for them, and re-layouts  21.5 us (2%)
  between operations  14 us (2%)
  starting transfers between devices  10.7 us (1%)
  other arithmetic  10.4 us (1%)
    ppermute x8, waiting for transfers between devices, swapped(): return lax.ppermute(block, axis, route)  597 us
    all_gather x1, waiting for transfers between devices, top_upper(): lax.all_gather(own_rows, 'leaf', axis=0, tiled=True)  109 us
    dot_general x3, matrix products, on_device(): jnp.dot(columns, upper_rows, preferred_element_type=jnp.float32)  36.5 us
    dot_general x3, matrix products, extend_add(): jnp.einsum('sb,brc->src', own_table, own_blocks, preferred_element_type=j...  30.1 us
    dot_general x3, matrix products, extend_add(): jnp.einsum('sb,brc->src', cross_table, cross_blocks, preferred_element_ty...  24.3 us
  transfers between devices with their start and end apart: 9, of which 9 were waited for; matrix products, arithmetic and copies ran while one was open for 5% of the time, Pallas kernels for 0%

profile of v1, /device:TPU:0, one launch (start us, length us, event | category | flops | bytes accessed | tf_op | source)
XLA Modules:
  0.0 860.1 jit_solution(9683163609040368817)
XLA Ops:
  6.5 3.0 collective-permute-start
  9.5 1.0 slice_reduce_fusion.5
  10.5 1.0 slice_reduce_fusion
  11.5 10.0 %fusion.28 = f32[2,128,8192]{2,0,1:T(2,128)S(1)} fusion(bf16[2,128,8192]{2,1,0:T(8,128)(2,1)} %bitcast.64, s32[2]{0:T(128)S(1)} %get-tuple-element.9), kind=kOutput, calls=%fused_computation.41 | convolution fusion | flops 8388612 | bytes 12582920 | tf_op jit(solution)/shard_map/sb,brc->src/dot_general | solution.py:32
  21.6 78.7 %collective-permute-done = bf16[256,8192]{1,0:T(8,128)(2,1)S(1)} collective-permute-done((bf16[256,8192]{1,0:T(8,128)(2,1)}, bf16[256,8192]{1,0:T(8,128)(2,1)S(1)}, u32[]{:S(2)}, u32[]{:S(2)}) %collective-permute-start) | collective-permute-done | bytes 4194336 | tf_op jit(solution)/shard_map/ppermute | solution.py:17
  100.3 8.1 fusion.3
  108.4 2.0 copy-done
  110.4 2.3 copy.35
  112.7 1.8 collective-permute-start.1
  114.5 45.2 %collective-permute-done.1 = bf16[128,8192]{1,0:T(8,128)(2,1)} collective-permute-done((bf16[128,8192]{1,0:T(8,128)(2,1)S(1)}, bf16[128,8192]{1,0:T(8,128)(2,1)}, u32[]{:S(2)}, u32[]{:S(2)}) %collective-permute-start.1) | collective-permute-done | bytes 2097184 | tf_op jit(solution)/shard_map/ppermute | solution.py:17
  159.7 4.5 maximum_select_fusion.8
  164.2 1.5 collective-permute-start.2
  165.7 4.9 copy.14
  170.6 2.0 copy-done.3
  172.6 2.4 all-gather
  175.0 0.1 reduce_sum.36
  175.1 80.4 %collective-permute-done.2 = bf16[256,8192]{1,0:T(8,128)(2,1)} collective-permute-done((bf16[256,8192]{1,0:T(8,128)(2,1)}, bf16[256,8192]{1,0:T(8,128)(2,1)}, u32[]{:S(2)}, u32[]{:S(2)}) %collective-permute-start.2) | collective-permute-done | bytes 4194336 | tf_op jit(solution)/shard_map/ppermute | solution.py:17
  255.4 12.5 %fusion.8 = bf16[256,8192]{1,0:T(8,128)(2,1)} fusion(bf16[256,512]{1,0:T(8,128)(2,1)S(1)} %reduce_sum.36, bf16[256,8192]{1,0:T(8,128)(2,1)} %bitcast.60, bf16[256,8192]{1,0:T(8,128)(2,1)} %maximum_select_fusion.8, bf16[256,8192]{1,0:T(8,128)(2,1)} %collective-permute-done.2, pred[]{:T(512)S(6)} %eq.123, pred[256]{0:T(512)(128)(4,1)S(1)} %iota_compare_fusion, ...), kind=kOutput, calls=%fused_computation.17 | convolution fusion | flops 6492782592 | bytes 17563908 | tf_op jit(solution)/shard_map/dot_general | solution.py:88
  267.9 1.2 collective-permute-start.3
  269.2 10.0 %fusion.25 = f32[2,128,8192]{2,0,1:T(2,128)S(1)} fusion(bf16[2,128,8192]{2,1,0:T(8,128)(2,1)} %bitcast.67, s32[2]{0:T(128)S(1)} %get-tuple-element.10), kind=kOutput, calls=%fused_computation.38 | convolution fusion | flops 8388612 | bytes 12582920 | tf_op jit(solution)/shard_map/sb,brc->src/dot_general | solution.py:32
  279.2 78.9 %collective-permute-done.3 = bf16[256,8192]{1,0:T(8,128)(2,1)S(1)} collective-permute-done((bf16[256,8192]{1,0:T(8,128)(2,1)}, bf16[256,8192]{1,0:T(8,128)(2,1)S(1)}, u32[]{:S(2)}, u32[]{:S(2)}) %collective-permute-start.3) | collective-permute-done | bytes 4194336 | tf_op jit(solution)/shard_map/ppermute | solution.py:17
  358.2 8.1 fusion.4
  366.3 2.7 copy.17
  369.0 0.1 slice.55
  369.0 0.9 collective-permute-start.4
  370.0 20.9 %collective-permute-done.4 = bf16[64,8192]{1,0:T(8,128)(2,1)S(1)} collective-permute-done((bf16[64,8192]{1,0:T(8,128)(2,1)S(1)}, bf16[64,8192]{1,0:T(8,128)(2,1)S(1)}, u32[]{:S(2)}, u32[]{:S(2)}) %collective-permute-start.4) | collective-permute-done | bytes 1048608 | tf_op jit(solution)/shard_map/ppermute | solution.py:17
  390.9 0.4 maximum_select_fusion.10
  391.3 0.7 collective-permute-start.5
  392.0 42.7 %collective-permute-done.5 = bf16[128,8192]{1,0:T(8,128)(2,1)S(1)} collective-permute-done((bf16[128,8192]{1,0:T(8,128)(2,1)S(1)}, bf16[128,8192]{1,0:T(8,128)(2,1)S(1)}, u32[]{:S(2)}, u32[]{:S(2)}) %collective-permute-start.5) | collective-permute-done | bytes 2097184 | tf_op jit(solution)/shard_map/ppermute | solution.py:17
  434.7 3.2 maximum_select_fusion.9
  437.9 0.4 collective-permute-start.6
  438.3 1.0 slice_select_fusion.1
  439.3 2.2 all-gather.1
  441.5 0.1 reduce_sum.37
  441.6 84.1 %collective-permute-done.6 = bf16[256,8192]{1,0:T(8,128)(2,1)} collective-permute-done((bf16[256,8192]{1,0:T(8,128)(2,1)}, bf16[256,8192]{1,0:T(8,128)(2,1)}, u32[]{:S(2)}, u32[]{:S(2)}) %collective-permute-start.6) | collective-permute-done | bytes 4194336 | tf_op jit(solution)/shard_map/ppermute | solution.py:17
  525.7 12.5 %fusion.7 = bf16[256,8192]{1,0:T(8,128)(2,1)} fusion(bf16[256,512]{1,0:T(8,128)(2,1)S(1)} %reduce_sum.37, bf16[256,8192]{1,0:T(8,128)(2,1)} %bitcast.55, bf16[256,8192]{1,0:T(8,128)(2,1)} %maximum_select_fusion.9, bf16[256,8192]{1,0:T(8,128)(2,1)} %collective-permute-done.6, pred[]{:T(512)S(6)} %eq.129, pred[256]{0:T(512)(128)(4,1)S(1)} %iota_compare_fusion.1, ...), kind=kOutput, calls=%fused_computation.16 | convolution fusion | flops 6492782592 | bytes 17563908 | tf_op jit(solution)/shard_map/dot_general | solution.py:88
  538.2 1.2 collective-permute-start.7
  539.4 10.0 %fusion.22 = f32[2,128,8192]{2,0,1:T(2,128)S(1)} fusion(bf16[2,128,8192]{2,1,0:T(8,128)(2,1)} %bitcast.66, s32[2]{0:T(128)S(1)} %get-tuple-element.8), kind=kOutput, calls=%fused_computation.35 | convolution fusion | flops 8388612 | bytes 12582920 | tf_op jit(solution)/shard_map/sb,brc->src/dot_general | solution.py:32
  549.4 166.0 %collective-permute-done.7 = bf16[256,8192]{1,0:T(8,128)(2,1)S(1)} collective-permute-done((bf16[256,8192]{1,0:T(8,128)(2,1)}, bf16[256,8192]{1,0:T(8,128)(2,1)S(1)}, u32[]{:S(2)}, u32[]{:S(2)}) %collective-permute-start.7) | collective-permute-done | bytes 4194336 | tf_op jit(solution)/shard_map/ppermute | solution.py:17
  715.4 8.1 fusion.5
  723.5 2.7 copy.20
  726.2 2.0 copy-done.2
  728.2 0.9 slice.57
  729.1 1.0 slice_select_fusion
  730.1 2.2 all-gather.2
  732.3 0.1 reduce_sum.38
  732.4 109.0 %all-gather.5.cloned.1.call-done = bf16[512,8192]{1,0:T(8,128)(2,1)} async-done(((bf16[32,8192]{1,0:T(8,128)(2,1)}), bf16[512,8192]{1,0:T(8,128)(2,1)}) %all-gather.5.cloned.1.call-update) | async-done | bytes 8388624 | tf_op jit(solution)/shard_map/all_gather | solution.py:55
  841.4 11.5 %fusion.6 = bf16[256,8192]{1,0:T(8,128)(2,1)} fusion(bf16[256,512]{1,0:T(8,128)(2,1)S(1)} %reduce_sum.38, bf16[256,8192]{1,0:T(8,128)(2,1)} %bitcast.58, pred[256]{0:T(512)(128)(4,1)S(1)} %iota_compare_fusion.2, bf16[512,8192]{1,0:T(8,128)(2,1)} %all-gather.5.cloned.1.call-done, bf16[7,512,512]{2,1,0:T(8,128)(2,1)} %param.7, s32[]{:T(128)S(6)} %select_n.104), kind=kOutput, calls=%fused_computation.15 | convolution fusion | flops 6455033856 | bytes 17563908 | tf_op jit(solution)/shard_map/dot_general | solution.py:88
  (11 shorter events, 0.1 us)
Async XLA Ops:
  6.5 834.8 %all-gather.5.cloned.1.call-start = ((), (), s32[]{:S(2)}) async-start(), calls=%async_computation | async-start | bytes 8912896 | tf_op jit(solution)/shard_map/all_gather | solution.py:55
  6.5 93.8 %collective-permute-start = (bf16[256,8192]{1,0:T(8,128)(2,1)}, bf16[256,8192]{1,0:T(8,128)(2,1)S(1)}, u32[]{:S(2)}, u32[]{:S(2)}) collective-permute-start(bf16[256,8192]{1,0:T(8,128)(2,1)} %param.4), channel_id=1, source_target_pairs={{0,4},{4,0},{2,6},{6,2},{8,12},{12,8},{10,14},{14,10},{16,20},{20,... | collective-permute-start | bytes 12582920 | tf_op jit(solution)/shard_map/ppermute | solution.py:17
  108.4 2.0 copy-start
  112.7 47.0 %collective-permute-start.1 = (bf16[128,8192]{1,0:T(8,128)(2,1)S(1)}, bf16[128,8192]{1,0:T(8,128)(2,1)}, u32[]{:S(2)}, u32[]{:S(2)}) collective-permute-start(bf16[128,8192]{1,0:T(8,128)(2,1)S(1)} %bitcast.51), channel_id=1, source_target_pairs={{0,2},{2,0},{4,6},{6,4},{8,10},{10,8},{12,14},{14,12},{16,18},{18,... | collective-permute-start | bytes 6291464 | tf_op jit(solution)/shard_map/ppermute | solution.py:17
  164.2 91.2 %collective-permute-start.2 = (bf16[256,8192]{1,0:T(8,128)(2,1)}, bf16[256,8192]{1,0:T(8,128)(2,1)}, u32[]{:S(2)}, u32[]{:S(2)}) collective-permute-start(bf16[256,8192]{1,0:T(8,128)(2,1)} %maximum_select_fusion.8), channel_id=1, source_target_pairs={{0,4},{4,0},{2,6},{6,2},{8,12},{12,8},{10,14},{14,10},{16,20},{20,... | collective-permute-start | bytes 12582920 | tf_op jit(solution)/shard_map/ppermute | solution.py:17
  170.6 2.0 copy-start.3
  267.9 90.2 %collective-permute-start.3 = (bf16[256,8192]{1,0:T(8,128)(2,1)}, bf16[256,8192]{1,0:T(8,128)(2,1)S(1)}, u32[]{:S(2)}, u32[]{:S(2)}) collective-permute-start(bf16[256,8192]{1,0:T(8,128)(2,1)} %fusion.8), channel_id=1, source_target_pairs={{0,8},{8,0},{2,10},{10,2},{4,12},{12,4},{6,14},{14,6},{16,24},{24,... | collective-permute-start | bytes 12582920 | tf_op jit(solution)/shard_map/ppermute | solution.py:17
  369.0 69.0 %copy-start.1 = (bf16[2,128,8192]{2,1,0:T(8,128)(2,1)}, bf16[2,128,8192]{2,1,0:T(8,128)(2,1)S(1)}, u32[]{:S(2)}) copy-start(bf16[2,128,8192]{2,1,0:T(8,128)(2,1)S(1)} %copy.17) | copy-start | bytes 12582916
  369.0 21.8 %collective-permute-start.4 = (bf16[64,8192]{1,0:T(8,128)(2,1)S(1)}, bf16[64,8192]{1,0:T(8,128)(2,1)S(1)}, u32[]{:S(2)}, u32[]{:S(2)}) collective-permute-start(bf16[64,8192]{1,0:T(8,128)(2,1)S(1)} %slice.55), channel_id=1, source_target_pairs={{0,2},{2,0},{4,6},{6,4},{8,10},{10,8},{12,14},{14,12},{16,18},{18,... | collective-permute-start | bytes 3145736 | tf_op jit(solution)/shard_map/ppermute | solution.py:17
  391.3 43.4 %collective-permute-start.5 = (bf16[128,8192]{1,0:T(8,128)(2,1)S(1)}, bf16[128,8192]{1,0:T(8,128)(2,1)S(1)}, u32[]{:S(2)}, u32[]{:S(2)}) collective-permute-start(bf16[128,8192]{1,0:T(8,128)(2,1)S(1)} %maximum_select_fusion.10), channel_id=1, source_target_pairs={{0,4},{4,0},{2,6},{6,2},{8,12},{12,8},{10,14},{14,10},{16,20},{20,... | collective-permute-start | bytes 6291464 | tf_op jit(solution)/shard_map/ppermute | solution.py:17
  437.9 87.8 %collective-permute-start.6 = (bf16[256,8192]{1,0:T(8,128)(2,1)}, bf16[256,8192]{1,0:T(8,128)(2,1)}, u32[]{:S(2)}, u32[]{:S(2)}) collective-permute-start(bf16[256,8192]{1,0:T(8,128)(2,1)} %maximum_select_fusion.9), channel_id=1, source_target_pairs={{0,8},{8,0},{2,10},{10,2},{4,12},{12,4},{6,14},{14,6},{16,24},{24,... | collective-permute-start | bytes 12582920 | tf_op jit(solution)/shard_map/ppermute | solution.py:17
  538.2 177.2 %collective-permute-start.7 = (bf16[256,8192]{1,0:T(8,128)(2,1)}, bf16[256,8192]{1,0:T(8,128)(2,1)S(1)}, u32[]{:S(2)}, u32[]{:S(2)}) collective-permute-start(bf16[256,8192]{1,0:T(8,128)(2,1)} %fusion.7), channel_id=1, source_target_pairs={{0,16},{16,0},{2,18},{18,2},{4,20},{20,4},{6,22},{22,6},{8,24},{24... | collective-permute-start | bytes 12582920 | tf_op jit(solution)/shard_map/ppermute | solution.py:17
  726.2 2.0 copy-start.2
Sparse Core Ops, SparseCore 0:
  729.2 112.0 all-gather.4
